TPU v7x, 32 devices: a whole 2x2x4 slice. The times are simulated.
32 devices in a mesh: row: 8 (over z, y), col: 4 (over x, core).
Axes of the slice: x: 2, y: 2, z: 4, core: 2. Of those that a mesh axis runs over, the one named last changes fastest.
Arguments:
- momentum: float32 [8192, 8192], P('row', 'col'), may hold values from -6 to 6
- gradient: bfloat16 [8192, 8192], P('row', 'col'), may hold values from -6 to 6
- weight: bfloat16 [8192, 8192], P('row', 'col'), may hold values from -6 to 6
- right_start: float32 [8192, 512], P('col', 'row'), may hold values from -0.0625 to 0.0625
Outputs:
- new_momentum: float32 [8192, 8192], P('row', 'col')
- new_weight: bfloat16 [8192, 8192], P('row', 'col')
- new_right: float32 [8192, 512], P('col', 'row')
All inputs are finite; a program needn't handle non-finite values.
Results may differ from a plain program's by a relative error of at most 0.001.
Values sent between devices are 32-bit elements; how exact they have to be, the bound alone decides.
A program may use at most 128 MiB of HBM per device.

v0:
```python
import jax
import jax.numpy as jnp
from jax import lax
from jax.sharding import PartitionSpec as P

ITERS = 2
BLOCK = 128
gram_mode = lax.Precision.HIGHEST
wide_mode = lax.Precision.HIGH
momentum_decay = 0.9
step_rate = 0.1
epsilon = 1e-06


def self_gram(rows):
    return lax.dot_general(rows, rows, (((0,), (0,)), ((), ())), precision=gram_mode)


def times_transposed(a, b):
    return lax.dot_general(a, b, (((1,), (1,)), ((), ())), precision=gram_mode)


def solve_rows(rows, gram_sum):
    rank = gram_sum.shape[0]
    block = min(BLOCK, rank)
    trailing = gram_sum
    rest = rows
    solved = []
    for at in range(0, rank, block):
        size = min(block, rank - at)
        corner = lax.linalg.cholesky(trailing[:size, :size], symmetrize_input=False)
        inverse = lax.linalg.triangular_solve(
            corner, jnp.eye(size, dtype=corner.dtype), left_side=True, lower=True
        )
        block_rows = times_transposed(rest[:, :size], inverse)
        solved.append(block_rows)
        if at + size < rank:
            panel = times_transposed(trailing[size:, :size], inverse)
            trailing = trailing[size:, size:] - times_transposed(panel, panel)
            rest = rest[:, size:] - times_transposed(block_rows, panel)
    return jnp.concatenate(solved, axis=1)


def shards(momentum, gradient, weight, right_start):
    rows_at, cols_at = (lax.psum(1, "row"), lax.psum(1, "col"))
    out_dim, in_dim = (momentum.shape[0] * rows_at, momentum.shape[1] * cols_at)
    rank = right_start.shape[1] * rows_at
    blended = momentum + gradient.astype(jnp.float32)
    right_full = lax.all_gather(right_start, "row", axis=1, tiled=True)
    right_shard = right_start
    for iteration in range(ITERS):
        partials = jnp.dot(blended, right_full, precision=wide_mode)
        left_sum = lax.psum(partials, "col")
        gram_sum = lax.psum(self_gram(left_sum), "row")
        left_rows = solve_rows(left_sum, gram_sum)
        transposed = lax.dot_general(
            blended, left_rows, (((0,), (0,)), ((), ())), precision=wide_mode
        )
        products = lax.psum_scatter(transposed, "row", scatter_dimension=1, tiled=True)
        squares = lax.psum(jnp.sum(products * products, axis=0, keepdims=True), "col")
        col_norms = jnp.sqrt(squares + epsilon)
        right_shard = products / col_norms
        products_full, norms_full = (
            lax.all_gather(products, "row", axis=1, tiled=True),
            lax.all_gather(col_norms, "row", axis=1, tiled=True),
        )
        right_full = products_full / norms_full
    outer_dims = (((1,), (1,)), ((), ()))
    feedback = lax.dot_general(left_rows, products_full, outer_dims, precision=wide_mode)
    new_momentum = blended - (1.0 - momentum_decay) * feedback
    scale_factor = step_rate * (out_dim * in_dim / rank) ** 0.5
    update = lax.dot_general(left_rows, right_full, outer_dims, precision=wide_mode)
    new_weight = (weight.astype(jnp.float32) - scale_factor * update).astype(jnp.bfloat16)
    return (new_momentum, new_weight, right_shard)


def solution(mesh):
    return jax.shard_map(
        shards,
        mesh=mesh,
        in_specs=(P("row", "col"), P("row", "col"), P("row", "col"), P("col", "row")),
        out_specs=(P("row", "col"), P("row", "col"), P("col", "row")),
        check_vma=False,
    )
```

profile of v0, /device:TPU:0, one launch (start us, length us, event | category | flops | bytes accessed | tf_op | source)
XLA Modules:
  0.0 969.1 jit_solution(15669869728964990464)
XLA Ops:
  7.2 0.7 all-gather.4.cloned.1.call-update
  7.9 77.7 %all-gather.4.cloned.1.call-done = f32[2048,512]{0,1:T(8,128)} async-done(((f32[2048,64]{0,1:T(8,128)}), f32[2048,512]{0,1:T(8,128)}) %all-gather.4.cloned.1.call-update) | async-done | bytes 4194320 | tf_op jit(solution)/shard_map/all_gather | solution.py:49
  85.7 12.0 %fusion.75 = f32[1024,512]{1,0:T(8,128)} fusion(f32[2048,512]{0,1:T(8,128)} %all-gather.4.cloned.1.call-done, f32[1024,2048]{1,0:T(8,128)} %param.7, bf16[1024,2048]{1,0:T(8,128)(2,1)} %param.8), kind=kOutput, calls=%fused_computation.122 | convolution fusion | flops 6446645248 | bytes 18874368 | tf_op jit(solution)/shard_map/dot_general | solution.py:52
  97.7 50.0 %all-reduce.7.cloned.1.call-done = f32[1024,512]{1,0:T(8,128)} async-done(((f32[1024,512]{1,0:T(8,128)}), f32[1024,512]{1,0:T(8,128)}) %all-reduce.7.cloned.1.call-update) | async-done | bytes 2097168 | tf_op jit(solution)/shard_map/psum | solution.py:53
  147.7 6.7 fusion.76
  154.7 78.3 %all-reduce.9.cloned.1.call-done = f32[512,512]{1,0:T(8,128)} async-done(((f32[512,512]{1,0:T(8,128)}), f32[512,512]{1,0:T(8,128)}) %all-reduce.9.cloned.1.call-update) | async-done | bytes 1048592 | tf_op jit(solution)/shard_map/psum | solution.py:54
  233.0 0.8 slice.125
  233.8 11.7 %custom-call.20 = f32[128,128]{1,0:T(8,128)S(1)} custom-call(f32[128,128]{1,0:T(8,128)S(1)} %slice.125), custom_call_target="Cholesky" | custom-call | tf_op jit(solution)/shard_map/cholesky/custom-call.1 | solution.py:31
  245.5 0.6 compare_reduce_fusion.7
  246.2 0.7 fusion.50
  246.9 9.8 %custom-call.21 = f32[1,128,128]{1,2,0:T(8,128)S(1)} custom-call(f32[1,128,128]{2,1,0:T(8,128)S(1)} %fusion.50), custom_call_target="InvertDiagBlocksLowerTriangular" | custom-call | tf_op jit(solution)/shard_map/triangular_solve/custom-call.0 | solution.py:32
  257.0 1.3 fusion.44
  258.2 1.7 convolution_subtract_fusion.3
  259.9 11.7 %custom-call.22 = f32[128,128]{1,0:T(8,128)S(1)} custom-call(f32[128,128]{1,0:T(8,128)S(1)} %slice.130), custom_call_target="Cholesky" | custom-call | tf_op jit(solution)/shard_map/cholesky/custom-call.1 | solution.py:31
  271.7 0.6 compare_reduce_fusion.6
  272.3 0.7 fusion.51
  273.0 10.2 %custom-call.23 = f32[1,128,128]{1,2,0:T(8,128)S(1)} custom-call(f32[1,128,128]{2,1,0:T(8,128)S(1)} %fusion.51), custom_call_target="InvertDiagBlocksLowerTriangular" | custom-call | tf_op jit(solution)/shard_map/triangular_solve/custom-call.0 | solution.py:32
  284.2 11.7 %custom-call.24 = f32[128,128]{1,0:T(8,128)S(1)} custom-call(f32[128,128]{1,0:T(8,128)S(1)} %slice.135), custom_call_target="Cholesky" | custom-call | tf_op jit(solution)/shard_map/cholesky/custom-call.1 | solution.py:31
  296.6 0.7 fusion.52
  297.2 9.8 %custom-call.25 = f32[1,128,128]{1,2,0:T(8,128)S(1)} custom-call(f32[1,128,128]{2,1,0:T(8,128)S(1)} %fusion.52), custom_call_target="InvertDiagBlocksLowerTriangular" | custom-call | tf_op jit(solution)/shard_map/triangular_solve/custom-call.0 | solution.py:32
  307.9 11.7 %custom-call.26 = f32[128,128]{1,0:T(8,128)S(1)} custom-call(f32[128,128]{1,0:T(8,128)S(1)} %convolution_subtract_fusion.9), custom_call_target="Cholesky" | custom-call | tf_op jit(solution)/shard_map/cholesky/custom-call.1 | solution.py:31
  320.3 0.7 fusion.53
  320.9 10.0 %custom-call.27 = f32[1,128,128]{1,2,0:T(8,128)S(1)} custom-call(f32[1,128,128]{2,1,0:T(8,128)S(1)} %fusion.53), custom_call_target="InvertDiagBlocksLowerTriangular" | custom-call | tf_op jit(solution)/shard_map/triangular_solve/custom-call.0 | solution.py:32
  331.8 1.9 slice_subtract_fusion.1
  334.4 1.1 convolution_subtract_fusion.1
  336.0 1.0 convolution_subtract_fusion.5
  337.7 11.1 %fusion.3 = f32[2048,512]{0,1:T(8,128)} fusion(f32[1024,128]{0,1:T(8,128)S(1)} %fusion.77, f32[1024,128]{0,1:T(8,128)S(1)} %fusion.19, f32[1024,128]{0,1:T(8,128)S(1)} %fusion.21, f32[1024,128]{0,1:T(8,128)S(1)} %fusion.23, f32[1024,2048]{1,0:T(8,128)} %param.7, bf16[1024,2048]{1,0:T(8,128)(2,1)S(1)} %copy-done), kind=kOutput, calls=%fused_computation.6 | convolution fusion | flops 6448218112 | bytes 18874368 | tf_op jit(solution)/shard_map/dot_general | solution.py:56
  348.8 88.0 %reduce-scatter.3.cloned.1.call-done = f32[2048,64]{0,1:T(8,128)} async-done(((f32[2048,512]{0,1:T(8,128)}), f32[2048,64]{0,1:T(8,128)}) %reduce-scatter.3.cloned.1.call-update) | async-done | bytes 524304 | tf_op jit(solution)/shard_map/reduce_scatter | solution.py:59
  438.1 1.2 multiply_reduce_fusion.1
  439.3 6.2 psum.44
  445.6 21.6 %all-reduce = f32[512]{0:T(512)S(1)} all-reduce(f32[512]{0:T(512)S(1)} %bitcast_dynamic-update-slice_fusion), channel_id=1, replica_groups=mesh['row'=8,'col'=4] {'row'}, use_global_device_ids=true, to_apply=%add | all-reduce | flops 512 | bytes 4096
  467.2 44.4 %all-gather.6.cloned.1.call-done = f32[2048,512]{0,1:T(8,128)} async-done(((f32[2048,64]{0,1:T(8,128)}), f32[2048,512]{0,1:T(8,128)}) %all-gather.6.cloned.1.call-update) | async-done | bytes 4194320 | tf_op jit(solution)/shard_map/all_gather | solution.py:64
  511.6 12.2 %fusion.1 = f32[1024,512]{1,0:T(8,128)} fusion(f32[2048,512]{0,1:T(8,128)} %all-gather.6.cloned.1.call-done, f32[512]{0:T(512)S(1)} %all-reduce, f32[1024,2048]{1,0:T(8,128)} %param.7, bf16[1024,2048]{1,0:T(8,128)(2,1)} %param.8), kind=kOutput, calls=%fused_computation.4 | convolution fusion | flops 6447693824 | bytes 18876416 | tf_op jit(solution)/shard_map/dot_general | solution.py:52
  523.8 50.0 %all-reduce.11.cloned.1.call-done = f32[1024,512]{1,0:T(8,128)} async-done(((f32[1024,512]{1,0:T(8,128)}), f32[1024,512]{1,0:T(8,128)}) %all-reduce.11.cloned.1.call-update) | async-done | bytes 2097168 | tf_op jit(solution)/shard_map/psum | solution.py:53
  573.8 6.7 fusion.78
  581.0 78.1 %all-reduce.13.cloned.1.call-done = f32[512,512]{1,0:T(8,128)} async-done(((f32[512,512]{1,0:T(8,128)}), f32[512,512]{1,0:T(8,128)}) %all-reduce.13.cloned.1.call-update) | async-done | bytes 1048592 | tf_op jit(solution)/shard_map/psum | solution.py:54
  659.0 0.8 slice.140
  659.9 11.7 %custom-call.28 = f32[128,128]{1,0:T(8,128)S(1)} custom-call(f32[128,128]{1,0:T(8,128)S(1)} %slice.140), custom_call_target="Cholesky" | custom-call | tf_op jit(solution)/shard_map/cholesky/custom-call.1 | solution.py:31
  672.3 0.7 fusion.54
  672.9 9.8 %custom-call.29 = f32[1,128,128]{1,2,0:T(8,128)S(1)} custom-call(f32[1,128,128]{2,1,0:T(8,128)S(1)} %fusion.54), custom_call_target="InvertDiagBlocksLowerTriangular" | custom-call | tf_op jit(solution)/shard_map/triangular_solve/custom-call.0 | solution.py:32
  683.1 1.3 fusion.42
  684.3 1.7 convolution_subtract_fusion.2
  686.1 11.7 %custom-call.30 = f32[128,128]{1,0:T(8,128)S(1)} custom-call(f32[128,128]{1,0:T(8,128)S(1)} %slice.145), custom_call_target="Cholesky" | custom-call | tf_op jit(solution)/shard_map/cholesky/custom-call.1 | solution.py:31
  698.4 0.7 fusion.55
  699.1 10.0 %custom-call.31 = f32[1,128,128]{1,2,0:T(8,128)S(1)} custom-call(f32[1,128,128]{2,1,0:T(8,128)S(1)} %fusion.55), custom_call_target="InvertDiagBlocksLowerTriangular" | custom-call | tf_op jit(solution)/shard_map/triangular_solve/custom-call.0 | solution.py:32
  710.7 11.7 %custom-call.32 = f32[128,128]{1,0:T(8,128)S(1)} custom-call(f32[128,128]{1,0:T(8,128)S(1)} %slice.150), custom_call_target="Cholesky" | custom-call | tf_op jit(solution)/shard_map/cholesky/custom-call.1 | solution.py:31
  722.5 0.6 compare_reduce_fusion.1
  723.7 9.8 %custom-call.33 = f32[1,128,128]{1,2,0:T(8,128)S(1)} custom-call(f32[1,128,128]{2,1,0:T(8,128)S(1)} %fusion.56), custom_call_target="InvertDiagBlocksLowerTriangular" | custom-call | tf_op jit(solution)/shard_map/triangular_solve/custom-call.0 | solution.py:32
  734.4 11.7 %custom-call.34 = f32[128,128]{1,0:T(8,128)S(1)} custom-call(f32[128,128]{1,0:T(8,128)S(1)} %convolution_subtract_fusion.8), custom_call_target="Cholesky" | custom-call | tf_op jit(solution)/shard_map/cholesky/custom-call.1 | solution.py:31
  746.1 0.6 compare_reduce_fusion
  747.6 9.8 %custom-call.35 = f32[1,128,128]{1,2,0:T(8,128)S(1)} custom-call(f32[1,128,128]{2,1,0:T(8,128)S(1)} %fusion.57), custom_call_target="InvertDiagBlocksLowerTriangular" | custom-call | tf_op jit(solution)/shard_map/triangular_solve/custom-call.0 | solution.py:32
  757.7 1.4 fusion.17
  759.2 1.9 slice_subtract_fusion
  761.7 1.0 convolution_subtract_fusion
  763.4 1.0 convolution_subtract_fusion.4
  765.0 10.9 %fusion.25 = f32[2048,512]{0,1:T(8,128)} fusion(f32[1024,128]{0,1:T(8,128)S(1)} %fusion.79, f32[1024,128]{0,1:T(8,128)S(1)} %fusion.13, f32[1024,128]{0,1:T(8,128)S(1)} %fusion.15, f32[1024,128]{0,1:T(8,128)S(1)} %fusion.17, f32[1024,2048]{1,0:T(8,128)} %param.7, bf16[1024,2048]{1,0:T(8,128)(2,1)S(1)} %copy-done.1), kind=kOutput, calls=%fused_computation.43 | convolution fusion | flops 6448218112 | bytes 18874368 | tf_op jit(solution)/shard_map/dot_general | solution.py:56
  776.0 88.0 %reduce-scatter.5.cloned.1.call-done = f32[2048,64]{0,1:T(8,128)} async-done(((f32[2048,512]{0,1:T(8,128)}), f32[2048,64]{0,1:T(8,128)}) %reduce-scatter.5.cloned.1.call-update) | async-done | bytes 524304 | tf_op jit(solution)/shard_map/reduce_scatter | solution.py:59
  864.0 1.2 multiply_reduce_fusion
  865.2 6.2 psum.47
  871.5 21.6 %all-reduce.1 = f32[512]{0:T(512)S(1)} all-reduce(f32[512]{0:T(512)S(1)} %fusion.74), channel_id=1, replica_groups=mesh['row'=8,'col'=4] {'row'}, use_global_device_ids=true, to_apply=%add.1 | all-reduce | flops 512 | bytes 4096
  893.1 1.9 broadcast_divide_fusion
  895.0 43.9 %all-gather.8.cloned.1.call-done = f32[2048,512]{0,1:T(8,128)} async-done(((f32[2048,64]{0,1:T(8,128)}), f32[2048,512]{0,1:T(8,128)}) %all-gather.8.cloned.1.call-update) | async-done | bytes 4194320 | tf_op jit(solution)/shard_map/all_gather | solution.py:64
  938.9 13.9 %multiply_subtract_fusion = f32[1024,2048]{1,0:T(8,128)} fusion(f32[2048,512]{0,1:T(8,128)} %all-gather.8.cloned.1.call-done, f32[1024,128]{0,1:T(8,128)S(1)} %fusion.79, f32[1024,128]{0,1:T(8,128)S(1)} %fusion.13, f32[1024,128]{0,1:T(8,128)S(1)} %fusion.15, f32[1024,128]{0,1:T(8,128)S(1)} %fusion.17, f32[1024,2048]{1,0:T(8,128)} %param.7, ...), kind=kOutput, calls=%fused_computation.1 | convolution fusion | flops 6452412416 | bytes 27262976 | tf_op jit(solution)/shard_map/dot_general | solution.py:69
  952.8 9.3 subtract_convert_fusion
  (84 shorter events, 15.6 us)
Async XLA Ops:
  7.2 78.5 %all-gather.4.cloned.1.call-start = ((), (), s32[]{:S(2)}) async-start(), calls=%async_computation.2 | async-start | bytes 4718592 | tf_op jit(solution)/shard_map/all_gather | solution.py:49
  7.9 139.8 %all-reduce.7.cloned.1.call-start = ((), (), s32[]{:S(2)}) async-start(), calls=%async_computation.3 | async-start | bytes 4194304 | tf_op jit(solution)/shard_map/psum | solution.py:53
  97.7 135.3 %all-reduce.9.cloned.1.call-start = ((), (), s32[]{:S(2)}) async-start(), calls=%async_computation.4 | async-start | bytes 2097152 | tf_op jit(solution)/shard_map/psum | solution.py:54
  154.4 176.8 %copy-start.2 = (f32[1024,512]{1,0:T(8,128)S(1)}, f32[1024,512]{1,0:T(8,128)}, u32[]{:S(2)}) copy-start(f32[1024,512]{1,0:T(8,128)} %all-reduce.7.cloned.1.call-done) | copy-start | bytes 6291460
  154.4 282.4 %reduce-scatter.3.cloned.1.call-start = ((), (), s32[]{:S(2)}) async-start(), calls=%async_computation.5 | async-start | bytes 4718592 | tf_op jit(solution)/shard_map/reduce_scatter | solution.py:59
  333.7 3.9 copy-start
  348.7 88.2 %copy-start.9 = (u32[32]{0:T(128)S(1)}, u32[32]{0:T(128)}, u32[]{:S(2)}) copy-start(u32[32]{0:T(128)} %constant.27) | copy-start | bytes 388
  348.8 162.8 %all-gather.6.cloned.1.call-start = ((), (), s32[]{:S(2)}) async-start(), calls=%async_computation.6 | async-start | bytes 4718592 | tf_op jit(solution)/shard_map/all_gather | solution.py:64
  436.8 137.0 %all-reduce.11.cloned.1.call-start = ((), (), s32[]{:S(2)}) async-start(), calls=%async_computation.7 | async-start | bytes 4194304 | tf_op jit(solution)/shard_map/psum | solution.py:53
  523.8 135.3 %all-reduce.13.cloned.1.call-start = ((), (), s32[]{:S(2)}) async-start(), calls=%async_computation.8 | async-start | bytes 2097152 | tf_op jit(solution)/shard_map/psum | solution.py:54
  580.5 177.2 %copy-start.3 = (f32[1024,512]{1,0:T(8,128)S(1)}, f32[1024,512]{1,0:T(8,128)}, u32[]{:S(2)}) copy-start(f32[1024,512]{1,0:T(8,128)} %all-reduce.11.cloned.1.call-done) | copy-start | bytes 6291460
  580.5 283.5 %reduce-scatter.5.cloned.1.call-start = ((), (), s32[]{:S(2)}) async-start(), calls=%async_computation.9 | async-start | bytes 4718592 | tf_op jit(solution)/shard_map/reduce_scatter | solution.py:59
  683.0 26.3 %copy-start.5 = (f32[128,128]{1,0:T(8,128)}, f32[128,128]{1,0:T(8,128)S(1)}, u32[]{:S(2)}) copy-start(f32[128,128]{1,0:T(8,128)S(1)} %fusion.32) | copy-start | bytes 196612
  709.4 0.6 copy-start.6
  710.7 50.4 %copy-start.7 = (f32[128,128]{1,0:T(8,128)S(1)}, f32[128,128]{1,0:T(8,128)}, u32[]{:S(2)}) copy-start(f32[128,128]{1,0:T(8,128)} %copy-done.6) | copy-start | bytes 196612
  761.1 3.9 copy-start.1
  775.9 162.9 %all-gather.8.cloned.1.call-start = ((), (), s32[]{:S(2)}) async-start(), calls=%async_computation.10 | async-start | bytes 4718592 | tf_op jit(solution)/shard_map/all_gather | solution.py:64
  938.9 13.9 %copy-start.4 = (f32[2048,512]{0,1:T(8,128)S(1)}, f32[2048,512]{0,1:T(8,128)}, u32[]{:S(2)}) copy-start(f32[2048,512]{0,1:T(8,128)} %all-gather.8.cloned.1.call-done) | copy-start | bytes 12582916
  938.9 13.9 %copy-start.8 = (bf16[1024,2048]{1,0:T(8,128)(2,1)S(1)}, bf16[1024,2048]{1,0:T(8,128)(2,1)}, u32[]{:S(2)}) copy-start(bf16[1024,2048]{1,0:T(8,128)(2,1)} %param.9) | copy-start | bytes 12582916
Sparse Core Ops, SparseCore 0:
  10.1 75.5 all-gather.3
  97.8 49.9 all-reduce.6
  154.5 78.3 all-reduce.8
  348.9 87.8 reduce-scatter.2
  438.8 72.7 all-gather.5
  523.9 49.8 all-reduce.10
  580.6 78.3 all-reduce.12
  776.0 87.8 reduce-scatter.4
  866.1 72.6 all-gather.7
where the time goes:
time: 975 us; the launch traced here: 969 us
  waiting for transfers between devices  599 us (61%)
  other arithmetic  188 us (19%)
  matrix products  107 us (11%)
  blocking collectives  55.5 us (6%)
  between operations  15.6 us (2%)
    reduce_scatter x2, waiting for transfers between devices, shards(): lax.psum_scatter(transposed, 'row', scatter_dimension=1, tiled=True)  176 us
    psum x2, waiting for transfers between devices, shards(): gram_sum = lax.psum(self_gram(left_sum), 'row')  156 us
    psum x2, waiting for transfers between devices, shards(): left_sum = lax.psum(partials, 'col')  100 us
    another operation x24, other arithmetic, solve_rows(): corner = lax.linalg.cholesky(trailing[:size, :size], symmetrize_input=False)  99.1 us
    all_gather x2, waiting for transfers between devices, shards(): lax.all_gather(products, 'row', axis=1, tiled=True)  88.2 us
    another operation x16, other arithmetic, solve_rows(): lax.linalg.triangular_solve(corner, jnp.eye(size, dtype=corner.dtype), le...  84.4 us
    all_gather x1, waiting for transfers between devices, shards(): right_full = lax.all_gather(right_start, 'row', axis=1, tiled=True)  77.7 us
    unnamed x2, blocking collectives  43.1 us
  transfers between devices with their start and end apart: 9, of which 9 were waited for; matrix products, arithmetic and copies ran while one was open for 1% of the time, Pallas kernels for 0%

commit v1 on v0

--- a/solution.py
+++ b/solution.py
@@ -50,7 +50,11 @@
     right_shard = right_start
     for iteration in range(ITERS):
         partials = jnp.dot(blended, right_full, precision=wide_mode)
-        left_sum = lax.psum(partials, "col")
+        left_sum = partials
+        for hop in (1, 2):
+            left_sum = left_sum + lax.ppermute(
+                left_sum, "col", [(dev, dev ^ hop) for dev in range(4)]
+            )
         gram_sum = lax.psum(self_gram(left_sum), "row")
         left_rows = solve_rows(left_sum, gram_sum)
         transposed = lax.dot_general(

time: 975 us -> 976 us (level)
    ppermute x0 -> x4, waiting for transfers between devices: none -> 101 us  [shards(): lax.ppermute(left_sum, 'col', [(dev, dev ^ hop) for dev in range(4)])]
    psum x2 -> x0, waiting for transfers between devices: 100 us -> none  [shards(): left_sum = lax.psum(partials, 'col')]
  transfers between devices with their start and end apart: 9 -> 11, of which waited for: 9 -> 11; matrix products, arithmetic and copies ran while one was open for 1% -> 1% of each run, Pallas kernels for 0% -> 0%
where the time goes in v1:
time: 976 us; the launch traced here: 968 us
  waiting for transfers between devices  597 us (61%)
  other arithmetic  190 us (19%)
  matrix products  101 us (10%)
  blocking collectives  55.5 us (6%)
  between operations  15.8 us (2%)
    reduce_scatter x2, waiting for transfers between devices, shards(): lax.psum_scatter(transposed, 'row', scatter_dimension=1, tiled=True)  176 us
    psum x2, waiting for transfers between devices, shards(): gram_sum = lax.psum(self_gram(left_sum), 'row')  153 us
    ppermute x4, waiting for transfers between devices, shards(): lax.ppermute(left_sum, 'col', [(dev, dev ^ hop) for dev in range(4)])  101 us
    another operation x24, other arithmetic, solve_rows(): corner = lax.linalg.cholesky(trailing[:size, :size], symmetrize_input=False)  99.5 us
    all_gather x2, waiting for transfers between devices, shards(): lax.all_gather(products, 'row', axis=1, tiled=True)  88.2 us
    another operation x16, other arithmetic, solve_rows(): lax.linalg.triangular_solve(corner, jnp.eye(size, dtype=corner.dtype), le...  84.3 us
    all_gather x1, waiting for transfers between devices, shards(): right_full = lax.all_gather(right_start, 'row', axis=1, tiled=True)  77.7 us
    unnamed x2, blocking collectives  43.2 us
  transfers between devices with their start and end apart: 11, of which 11 were waited for; matrix products, arithmetic and copies ran while one was open for 1% of the time, Pallas kernels for 0%

profile of v1, /device:TPU:0, one launch (start us, length us, event | category | flops | bytes accessed | tf_op | source)
XLA Modules:
  0.0 968.5 jit_solution(9608625235965745001)
XLA Ops:
  7.2 0.7 all-gather.4.cloned.1.call-update
  7.9 77.7 %all-gather.4.cloned.1.call-done = f32[2048,512]{0,1:T(8,128)} async-done(((f32[2048,64]{0,1:T(8,128)}), f32[2048,512]{0,1:T(8,128)}) %all-gather.4.cloned.1.call-update) | async-done | bytes 4194320 | tf_op jit(solution)/shard_map/all_gather | solution.py:49
  85.7 11.0 %fusion.77 = f32[1024,512]{1,0:T(8,128)S(1)} fusion(f32[2048,512]{0,1:T(8,128)} %all-gather.4.cloned.1.call-done, f32[1024,2048]{1,0:T(8,128)} %param.7, bf16[1024,2048]{1,0:T(8,128)(2,1)} %param.8), kind=kOutput, calls=%fused_computation.124 | convolution fusion | flops 6446645248 | bytes 18874368 | tf_op jit(solution)/shard_map/dot_general | solution.py:52
  96.8 4.1 collective-permute-done
  101.4 1.5 collective-permute-start.1
  102.9 46.2 %collective-permute-done.1 = f32[1024,512]{1,0:T(8,128)S(1)} collective-permute-done((f32[1024,512]{1,0:T(8,128)S(1)}, f32[1024,512]{1,0:T(8,128)S(1)}, u32[]{:S(2)}, u32[]{:S(2)}) %collective-permute-start.1) | collective-permute-done | bytes 2097184 | tf_op jit(solution)/shard_map/ppermute | solution.py:55
  149.6 4.5 fusion.78
  154.4 76.8 %all-reduce.5.cloned.1.call-done = f32[512,512]{1,0:T(8,128)} async-done(((f32[512,512]{1,0:T(8,128)}), f32[512,512]{1,0:T(8,128)}) %all-reduce.5.cloned.1.call-update) | async-done | bytes 1048592 | tf_op jit(solution)/shard_map/psum | solution.py:58
  231.2 0.8 slice.125
  232.0 11.7 %custom-call.20 = f32[128,128]{1,0:T(8,128)S(1)} custom-call(f32[128,128]{1,0:T(8,128)S(1)} %slice.125), custom_call_target="Cholesky" | custom-call | tf_op jit(solution)/shard_map/cholesky/custom-call.1 | solution.py:31
  244.4 0.7 fusion.52
  245.1 9.8 %custom-call.21 = f32[1,128,128]{1,2,0:T(8,128)S(1)} custom-call(f32[1,128,128]{2,1,0:T(8,128)S(1)} %fusion.52), custom_call_target="InvertDiagBlocksLowerTriangular" | custom-call | tf_op jit(solution)/shard_map/triangular_solve/custom-call.0 | solution.py:32
  255.8 1.3 fusion.46
  257.8 11.7 %custom-call.22 = f32[128,128]{1,0:T(8,128)S(1)} custom-call(f32[128,128]{1,0:T(8,128)S(1)} %slice.130), custom_call_target="Cholesky" | custom-call | tf_op jit(solution)/shard_map/cholesky/custom-call.1 | solution.py:31
  270.8 10.2 %custom-call.23 = f32[1,128,128]{1,2,0:T(8,128)S(1)} custom-call(f32[1,128,128]{2,1,0:T(8,128)S(1)} %fusion.53), custom_call_target="InvertDiagBlocksLowerTriangular" | custom-call | tf_op jit(solution)/shard_map/triangular_solve/custom-call.0 | solution.py:32
  282.6 0.7 copy-done.3
  283.3 11.7 %custom-call.24 = f32[128,128]{1,0:T(8,128)S(1)} custom-call(f32[128,128]{1,0:T(8,128)S(1)} %slice.135), custom_call_target="Cholesky" | custom-call | tf_op jit(solution)/shard_map/cholesky/custom-call.1 | solution.py:31
  296.4 9.8 %custom-call.25 = f32[1,128,128]{1,2,0:T(8,128)S(1)} custom-call(f32[1,128,128]{2,1,0:T(8,128)S(1)} %fusion.54), custom_call_target="InvertDiagBlocksLowerTriangular" | custom-call | tf_op jit(solution)/shard_map/triangular_solve/custom-call.0 | solution.py:32
  306.5 1.1 fusion.62
  307.6 1.1 convolution_subtract_fusion.3
  308.7 11.9 %custom-call.26 = f32[128,128]{1,0:T(8,128)S(1)} custom-call(f32[128,128]{1,0:T(8,128)S(1)} %convolution_subtract_fusion.3), custom_call_target="Cholesky" | custom-call | tf_op jit(solution)/shard_map/cholesky/custom-call.1 | solution.py:31
  321.9 9.8 %custom-call.27 = f32[1,128,128]{1,2,0:T(8,128)S(1)} custom-call(f32[1,128,128]{2,1,0:T(8,128)S(1)} %fusion.55), custom_call_target="InvertDiagBlocksLowerTriangular" | custom-call | tf_op jit(solution)/shard_map/triangular_solve/custom-call.0 | solution.py:32
  332.0 1.9 slice_subtract_fusion.1
  334.6 1.0 slice_subtract_fusion.3
  336.2 1.0 fusion.79
  337.9 11.0 %fusion.3 = f32[2048,512]{0,1:T(8,128)} fusion(f32[1024,128]{0,1:T(8,128)S(1)} %fusion.20, f32[1024,128]{0,1:T(8,128)S(1)} %fusion.21, f32[1024,128]{0,1:T(8,128)S(1)} %fusion.23, f32[1024,128]{0,1:T(8,128)S(1)} %fusion.25, f32[1024,2048]{1,0:T(8,128)} %param.7, bf16[1024,2048]{1,0:T(8,128)(2,1)S(1)} %copy-done), kind=kOutput, calls=%fused_computation.6 | convolution fusion | flops 6448218112 | bytes 18874368 | tf_op jit(solution)/shard_map/dot_general | solution.py:60
  349.0 88.0 %reduce-scatter.3.cloned.1.call-done = f32[2048,64]{0,1:T(8,128)} async-done(((f32[2048,512]{0,1:T(8,128)}), f32[2048,64]{0,1:T(8,128)}) %reduce-scatter.3.cloned.1.call-update) | async-done | bytes 524304 | tf_op jit(solution)/shard_map/reduce_scatter | solution.py:63
  438.3 1.2 multiply_reduce_fusion.1
  439.5 6.2 psum.29
  445.8 21.6 %all-reduce = f32[512]{0:T(512)S(1)} all-reduce(f32[512]{0:T(512)S(1)} %bitcast_dynamic-update-slice_fusion), channel_id=1, replica_groups=mesh['row'=8,'col'=4] {'row'}, use_global_device_ids=true, to_apply=%add | all-reduce | flops 512 | bytes 4096
  467.3 44.4 %all-gather.6.cloned.1.call-done = f32[2048,512]{0,1:T(8,128)} async-done(((f32[2048,64]{0,1:T(8,128)}), f32[2048,512]{0,1:T(8,128)}) %all-gather.6.cloned.1.call-update) | async-done | bytes 4194320 | tf_op jit(solution)/shard_map/all_gather | solution.py:68
  511.7 11.2 %fusion.1 = f32[1024,512]{1,0:T(8,128)S(1)} fusion(f32[2048,512]{0,1:T(8,128)} %all-gather.6.cloned.1.call-done, f32[512]{0:T(512)S(1)} %all-reduce, f32[1024,2048]{1,0:T(8,128)} %param.7, bf16[1024,2048]{1,0:T(8,128)(2,1)} %param.8), kind=kOutput, calls=%fused_computation.4 | convolution fusion | flops 6447693824 | bytes 18876416 | tf_op jit(solution)/shard_map/dot_general | solution.py:52
  523.0 4.1 collective-permute-done.2
  527.7 1.5 collective-permute-start.3
  529.2 46.2 %collective-permute-done.3 = f32[1024,512]{1,0:T(8,128)S(1)} collective-permute-done((f32[1024,512]{1,0:T(8,128)S(1)}, f32[1024,512]{1,0:T(8,128)S(1)}, u32[]{:S(2)}, u32[]{:S(2)}) %collective-permute-start.3) | collective-permute-done | bytes 2097184 | tf_op jit(solution)/shard_map/ppermute | solution.py:55
  575.9 4.5 fusion.80
  580.9 76.6 %all-reduce.7.cloned.1.call-done = f32[512,512]{1,0:T(8,128)} async-done(((f32[512,512]{1,0:T(8,128)}), f32[512,512]{1,0:T(8,128)}) %all-reduce.7.cloned.1.call-update) | async-done | bytes 1048592 | tf_op jit(solution)/shard_map/psum | solution.py:58
  657.5 0.8 slice.140
  658.3 11.7 %custom-call.28 = f32[128,128]{1,0:T(8,128)S(1)} custom-call(f32[128,128]{1,0:T(8,128)S(1)} %slice.140), custom_call_target="Cholesky" | custom-call | tf_op jit(solution)/shard_map/cholesky/custom-call.1 | solution.py:31
  671.4 9.8 %custom-call.29 = f32[1,128,128]{1,2,0:T(8,128)S(1)} custom-call(f32[1,128,128]{2,1,0:T(8,128)S(1)} %fusion.56), custom_call_target="InvertDiagBlocksLowerTriangular" | custom-call | tf_op jit(solution)/shard_map/triangular_solve/custom-call.0 | solution.py:32
  682.1 1.3 fusion.44
  684.0 11.7 %custom-call.30 = f32[128,128]{1,0:T(8,128)S(1)} custom-call(f32[128,128]{1,0:T(8,128)S(1)} %slice.145), custom_call_target="Cholesky" | custom-call | tf_op jit(solution)/shard_map/cholesky/custom-call.1 | solution.py:31
  697.1 10.0 %custom-call.31 = f32[1,128,128]{1,2,0:T(8,128)S(1)} custom-call(f32[1,128,128]{2,1,0:T(8,128)S(1)} %fusion.57), custom_call_target="InvertDiagBlocksLowerTriangular" | custom-call | tf_op jit(solution)/shard_map/triangular_solve/custom-call.0 | solution.py:32
  708.6 0.7 copy-done.4
  709.3 11.7 %custom-call.32 = f32[128,128]{1,0:T(8,128)S(1)} custom-call(f32[128,128]{1,0:T(8,128)S(1)} %slice.150), custom_call_target="Cholesky" | custom-call | tf_op jit(solution)/shard_map/cholesky/custom-call.1 | solution.py:31
  721.1 0.7 compare_reduce_fusion.1
  721.8 0.7 fusion.58
  722.5 9.8 %custom-call.33 = f32[1,128,128]{1,2,0:T(8,128)S(1)} custom-call(f32[1,128,128]{2,1,0:T(8,128)S(1)} %fusion.58), custom_call_target="InvertDiagBlocksLowerTriangular" | custom-call | tf_op jit(solution)/shard_map/triangular_solve/custom-call.0 | solution.py:32
  732.6 1.1 fusion.60
  733.7 1.1 convolution_subtract_fusion.2
  734.9 11.9 %custom-call.34 = f32[128,128]{1,0:T(8,128)S(1)} custom-call(f32[128,128]{1,0:T(8,128)S(1)} %convolution_subtract_fusion.2), custom_call_target="Cholesky" | custom-call | tf_op jit(solution)/shard_map/cholesky/custom-call.1 | solution.py:31
  748.1 9.8 %custom-call.35 = f32[1,128,128]{1,2,0:T(8,128)S(1)} custom-call(f32[1,128,128]{2,1,0:T(8,128)S(1)} %fusion.59), custom_call_target="InvertDiagBlocksLowerTriangular" | custom-call | tf_op jit(solution)/shard_map/triangular_solve/custom-call.0 | solution.py:32
  758.2 1.9 slice_subtract_fusion
  760.8 1.0 slice_subtract_fusion.2
  762.4 1.0 fusion.81
  764.1 10.9 %fusion.27 = f32[2048,512]{0,1:T(8,128)} fusion(f32[1024,128]{0,1:T(8,128)S(1)} %fusion.13, f32[1024,128]{0,1:T(8,128)S(1)} %fusion.14, f32[1024,128]{0,1:T(8,128)S(1)} %fusion.16, f32[1024,128]{0,1:T(8,128)S(1)} %fusion.18, f32[1024,2048]{1,0:T(8,128)} %param.7, bf16[1024,2048]{1,0:T(8,128)(2,1)S(1)} %copy-done.1), kind=kOutput, calls=%fused_computation.45 | convolution fusion | flops 6448218112 | bytes 18874368 | tf_op jit(solution)/shard_map/dot_general | solution.py:60
  775.0 88.0 %reduce-scatter.5.cloned.1.call-done = f32[2048,64]{0,1:T(8,128)} async-done(((f32[2048,512]{0,1:T(8,128)}), f32[2048,64]{0,1:T(8,128)}) %reduce-scatter.5.cloned.1.call-update) | async-done | bytes 524304 | tf_op jit(solution)/shard_map/reduce_scatter | solution.py:63
  863.1 1.2 multiply_reduce_fusion
  864.3 6.2 psum.31
  870.5 21.6 %all-reduce.1 = f32[512]{0:T(512)S(1)} all-reduce(f32[512]{0:T(512)S(1)} %fusion.76), channel_id=1, replica_groups=mesh['row'=8,'col'=4] {'row'}, use_global_device_ids=true, to_apply=%add.1 | all-reduce | flops 512 | bytes 4096
  892.1 1.9 broadcast_divide_fusion
  894.1 43.8 %all-gather.8.cloned.1.call-done = f32[2048,512]{0,1:T(8,128)} async-done(((f32[2048,64]{0,1:T(8,128)}), f32[2048,512]{0,1:T(8,128)}) %all-gather.8.cloned.1.call-update) | async-done | bytes 4194320 | tf_op jit(solution)/shard_map/all_gather | solution.py:68
  937.9 13.9 %multiply_subtract_fusion = f32[1024,2048]{1,0:T(8,128)} fusion(f32[2048,512]{0,1:T(8,128)} %all-gather.8.cloned.1.call-done, f32[1024,128]{0,1:T(8,128)S(1)} %fusion.13, f32[1024,128]{0,1:T(8,128)S(1)} %fusion.14, f32[1024,128]{0,1:T(8,128)S(1)} %fusion.16, f32[1024,128]{0,1:T(8,128)S(1)} %fusion.18, f32[1024,2048]{1,0:T(8,128)} %param.7, ...), kind=kOutput, calls=%fused_computation.1 | convolution fusion | flops 6452412416 | bytes 27262976 | tf_op jit(solution)/shard_map/dot_general | solution.py:73
  951.9 9.3 subtract_convert_fusion
  (96 shorter events, 23.7 us)
Async XLA Ops:
  7.2 78.5 %all-gather.4.cloned.1.call-start = ((), (), s32[]{:S(2)}) async-start(), calls=%async_computation.2 | async-start | bytes 4718592 | tf_op jit(solution)/shard_map/all_gather | solution.py:49
  7.9 223.3 %all-reduce.5.cloned.1.call-start = ((), (), s32[]{:S(2)}) async-start(), calls=%async_computation.3 | async-start | bytes 2097152 | tf_op jit(solution)/shard_map/psum | solution.py:58
  96.7 4.2 collective-permute-start
  101.4 47.7 %collective-permute-start.1 = (f32[1024,512]{1,0:T(8,128)S(1)}, f32[1024,512]{1,0:T(8,128)S(1)}, u32[]{:S(2)}, u32[]{:S(2)}) collective-permute-start(f32[1024,512]{1,0:T(8,128)S(1)} %add.38), channel_id=1, source_target_pairs={{0,2},{1,3},{2,0},{3,1},{4,6},{5,7},{6,4},{7,5},{8,10},{9,11},{10,... | collective-permute-start | bytes 6291464 | tf_op jit(solution)/shard_map/ppermute | solution.py:55
  154.1 282.9 %reduce-scatter.3.cloned.1.call-start = ((), (), s32[]{:S(2)}) async-start(), calls=%async_computation.4 | async-start | bytes 4718592 | tf_op jit(solution)/shard_map/reduce_scatter | solution.py:63
  254.9 2.2 copy-start.5
  281.3 0.6 copy-start.7
  282.6 0.7 copy-start.3
  320.6 13.4 %copy-start.8 = (f32[128,128]{1,0:T(8,128)S(1)}, f32[128,128]{1,0:T(8,128)}, u32[]{:S(2)}) copy-start(f32[128,128]{1,0:T(8,128)} %copy-done.7) | copy-start | bytes 196612
  334.5 3.3 copy-start
  348.9 88.2 %copy-start.12 = (u32[32]{0:T(128)S(1)}, u32[32]{0:T(128)}, u32[]{:S(2)}) copy-start(u32[32]{0:T(128)} %constant.27) | copy-start | bytes 388
  348.9 162.8 %all-gather.6.cloned.1.call-start = ((), (), s32[]{:S(2)}) async-start(), calls=%async_computation.5 | async-start | bytes 4718592 | tf_op jit(solution)/shard_map/all_gather | solution.py:68
  437.0 220.5 %all-reduce.7.cloned.1.call-start = ((), (), s32[]{:S(2)}) async-start(), calls=%async_computation.6 | async-start | bytes 2097152 | tf_op jit(solution)/shard_map/psum | solution.py:58
  523.0 4.2 collective-permute-start.2
  527.7 47.7 %collective-permute-start.3 = (f32[1024,512]{1,0:T(8,128)S(1)}, f32[1024,512]{1,0:T(8,128)S(1)}, u32[]{:S(2)}, u32[]{:S(2)}) collective-permute-start(f32[1024,512]{1,0:T(8,128)S(1)} %add.41), channel_id=1, source_target_pairs={{0,2},{1,3},{2,0},{3,1},{4,6},{5,7},{6,4},{7,5},{8,10},{9,11},{10,... | collective-permute-start | bytes 6291464 | tf_op jit(solution)/shard_map/ppermute | solution.py:55
  580.4 282.7 %reduce-scatter.5.cloned.1.call-start = ((), (), s32[]{:S(2)}) async-start(), calls=%async_computation.7 | async-start | bytes 4718592 | tf_op jit(solution)/shard_map/reduce_scatter | solution.py:63
  681.2 2.2 copy-start.6
  707.3 0.6 copy-start.9
  708.6 0.7 copy-start.4
  746.8 13.4 %copy-start.10 = (f32[128,128]{1,0:T(8,128)S(1)}, f32[128,128]{1,0:T(8,128)}, u32[]{:S(2)}) copy-start(f32[128,128]{1,0:T(8,128)} %copy-done.9) | copy-start | bytes 196612
  760.7 3.3 copy-start.1
  775.0 162.9 %all-gather.8.cloned.1.call-start = ((), (), s32[]{:S(2)}) async-start(), calls=%async_computation.8 | async-start | bytes 4718592 | tf_op jit(solution)/shard_map/all_gather | solution.py:68
  937.9 14.0 %copy-start.2 = (f32[2048,512]{0,1:T(8,128)S(1)}, f32[2048,512]{0,1:T(8,128)}, u32[]{:S(2)}) copy-start(f32[2048,512]{0,1:T(8,128)} %all-gather.8.cloned.1.call-done) | copy-start | bytes 12582916
  937.9 14.0 %copy-start.11 = (bf16[1024,2048]{1,0:T(8,128)(2,1)S(1)}, bf16[1024,2048]{1,0:T(8,128)(2,1)}, u32[]{:S(2)}) copy-start(bf16[1024,2048]{1,0:T(8,128)(2,1)} %param.9) | copy-start | bytes 12582916
Sparse Core Ops, SparseCore 0:
  10.1 75.5 all-gather.3
  154.2 76.8 all-reduce.4
  349.0 87.8 reduce-scatter.2
  439.0 72.7 all-gather.5
  580.5 76.8 all-reduce.6
  775.1 87.8 reduce-scatter.4
  865.2 72.6 all-gather.7
